TPU v7x, 512 devices: a whole 4x4x16 slice. The times are simulated.
512 devices in a mesh: node: 64 (over y, z), local: 8 (over x, core).
Axes of the slice: x: 4, y: 4, z: 16, core: 2. Of those that a mesh axis runs over, the one named last changes fastest.
Arguments:
- grad_out: bfloat16 [65536, 3584], P(('node', 'local')), may hold values from -6 to 6
- expert_ids: int32 [65536, 8], P(('node', 'local')), may hold values from 0 to 255, as said below
- gate_weights: float32 [65536, 8], P(('node', 'local')), may hold values from 0.05 to 0.35
- saved_hidden: bfloat16 [64, 1024, 1024], P('node', None, 'local'), may hold values from -0.59765625 to 0.59765625
- down_weight: bfloat16 [64, 1024, 3584], P('node', 'local'), may hold values from -0.1875 to 0.1875
- second_moment: bfloat16 [64, 1024, 3584], P('node', 'local'), may hold values from 0.0019989014 to 0.25
Outputs:
- gate_weight_gradient: float32 [65536, 8], P(('node', 'local'))
- hidden_grad: bfloat16 [64, 1024, 1024], P('node', None, 'local')
- new_weight: bfloat16 [64, 1024, 3584], P('node', 'local')
- new_second: bfloat16 [64, 1024, 3584], P('node', 'local')
Inputs may be any that keep to these rules, and one draw needn't show every extreme that they name: `expert_ids`: each row names 8 different experts on at most 4 nodes (node = id // 4), two on each; at most one per row is in flight (id % 4 == 0). Among the rows of one device at most 2 name the in-flight expert of any one node, and in every draw some node receives exactly 2 from every device.
All inputs are finite; a program needn't handle non-finite values.
Results may differ from a plain program's by a relative error of at most 0.0051.
Values may be sent and summed in bfloat16 or wider, within the bound.
No kernel may reach another device: no remote copies, remote signals or barrier semaphores. Data moves between devices by JAX's collectives and lax.ppermute only.
A program may use at most 128 MiB of HBM per device.

v0:
```python
import jax
import jax.numpy as jnp
from jax import lax
from jax.sharding import PartitionSpec as P

EXPERTS_PER_HOST = 4
CAP = 2
beta_second = 0.95
learn_rate = 0.002
decay_rate = 0.1
epsilon = 1e-08
correct_second = 0.994079470779666


def route(picked_experts, gate_values, node_count):
    transit_rows = picked_experts % EXPERTS_PER_HOST == 0
    row_present = jnp.any(transit_rows, 1)
    destination_node = jnp.sum(jnp.where(transit_rows, picked_experts // EXPERTS_PER_HOST, 0), 1)
    tokens = picked_experts.shape[0]
    same = (
        (destination_node[:, None] == destination_node[None, :])
        & row_present[None, :]
        & (jnp.arange(tokens)[None, :] < jnp.arange(tokens)[:, None])
    )
    within_rank = jnp.sum(same.astype(jnp.int32), 1)
    slot_index = destination_node * CAP + within_rank
    expert_location = (
        jnp.arange(node_count * CAP, dtype=jnp.int32)[:, None] == slot_index[None, :]
    ) & row_present[None, :]
    matched_gate = jnp.sum(jnp.where(transit_rows, gate_values, 0.0), 1).astype(jnp.bfloat16)
    return (expert_location, transit_rows, row_present, matched_gate.astype(jnp.float32))


def on_device(grad_out, expert_ids, gate_weights, saved_hidden, down_weight, second_moment):
    node_count = lax.axis_size("node")
    members = lax.axis_size("local")
    feature_count = grad_out.shape[1]
    expert_location, transit_rows, row_present, gate = route(expert_ids, gate_weights, node_count)
    slot_gate = jnp.sum(jnp.where(expert_location, gate[None, :], 0.0), 1)
    picked = jnp.dot(
        expert_location.astype(jnp.bfloat16), grad_out, preferred_element_type=jnp.float32
    )
    scaled_out = (slot_gate[:, None] * picked).astype(jnp.bfloat16)
    arrived = lax.all_to_all(
        scaled_out.reshape(node_count, CAP, feature_count),
        "node",
        split_axis=0,
        concat_axis=0,
        tiled=True,
    )
    scaled = lax.all_gather(
        arrived.reshape(node_count * CAP, feature_count), "local", axis=0, tiled=True
    )
    weight_now = down_weight[0]
    hidden_now = saved_hidden[0]
    hidden_f = lax.dot_general(
        scaled, weight_now, (((1,), (1,)), ((), ())), preferred_element_type=jnp.float32
    )
    slot_score = jnp.sum(hidden_f * hidden_now.astype(jnp.float32), 1)
    grad = lax.dot_general(
        hidden_now, scaled, (((0,), (0,)), ((), ())), preferred_element_type=jnp.float32
    )
    second_new = (
        beta_second * second_moment[0].astype(jnp.float32) + (1.0 - beta_second) * grad * grad
    )
    weight_f = weight_now.astype(jnp.float32)
    update = grad / (jnp.sqrt(second_new / correct_second) + epsilon) + decay_rate * weight_f
    weight_new = weight_f - learn_rate * update
    score_terms = slot_score.reshape(members, node_count * CAP)
    summed = lax.psum(score_terms, "local")
    own_terms = lax.dynamic_slice_in_dim(summed, lax.axis_index("local"), 1, 0)
    returned = lax.all_to_all(
        own_terms.reshape(node_count, CAP), "node", split_axis=0, concat_axis=0, tiled=True
    )
    returned_flat = returned.reshape(node_count * CAP)
    token_score = jnp.sum(jnp.where(expert_location, returned_flat[:, None], 0.0), 0)
    token_gradient = jnp.where(row_present, token_score / jnp.where(row_present, gate, 1.0), 0.0)
    gate_weight_gradient = jnp.where(transit_rows, token_gradient[:, None], 0.0)
    return (
        gate_weight_gradient,
        hidden_f.astype(jnp.bfloat16)[None],
        weight_new.astype(jnp.bfloat16)[None],
        second_new.astype(jnp.bfloat16)[None],
    )


def solution(mesh):
    return jax.shard_map(
        on_device,
        mesh=mesh,
        in_specs=(
            P(("node", "local"), None),
            P(("node", "local"), None),
            P(("node", "local"), None),
            P("node", None, "local"),
            P("node", "local", None),
            P("node", "local", None),
        ),
        out_specs=(
            P(("node", "local"), None),
            P("node", None, "local"),
            P("node", "local", None),
            P("node", "local", None),
        ),
        check_vma=False,
    )
```

profile of v0, /device:TPU:8, one launch (start us, length us, event | category | flops | bytes accessed | tf_op | source)
XLA Modules:
  0.0 181.2 jit_solution(6624401985966689629)
XLA Ops:
  7.2 0.0 copy-start
  7.2 0.0 all-gather.2.cloned.1.call-start
  7.2 0.8 fusion.18
  8.0 0.7 select_reduce_fusion.2
  8.7 0.0 copy-start.5
  8.7 0.2 convert_reduce_fusion
  8.9 0.1 select_reduce_fusion.1
  9.0 0.3 copy-done.5
  9.3 0.0 copy-done
  9.3 0.4 fusion
  9.7 0.3 reshape.51
  10.1 66.9 %all_to_all.14 = bf16[64,2,3584]{2,1,0:T(2,128)(2,1)S(1)} all-to-all(bf16[64,2,3584]{2,1,0:T(2,128)(2,1)S(1)} %reshape.51), channel_id=1, replica_groups=mesh['node'=64,'local'=8] {'node'}, dimensions={0} | all-to-all | bytes 1835008 | tf_op jit(solution)/shard_map/all_to_all | solution.py:44
  77.0 0.0 copy-start.4
  77.0 0.0 copy-start.1
  77.0 1.3 reshape.52
  78.3 0.0 copy-start.2
  78.3 0.0 all-gather.2.cloned.1.call-update
  78.3 0.0 copy-done.4
  78.3 0.1 copy.30
  78.5 0.0 copy-done.1
  78.5 1.3 copy.32
  79.7 0.0 copy-done.2
  79.7 1.3 copy.29
  81.0 0.0 copy-start.3
  81.0 42.7 %all-gather.2.cloned.1.call-done = bf16[1024,3584]{1,0:T(8,128)(2,1)} async-done(((bf16[128,3584]{1,0:T(8,128)(2,1)}), bf16[1024,3584]{1,0:T(8,128)(2,1)}) %all-gather.2.cloned.1.call-update) | async-done | bytes 7340048 | tf_op jit(solution)/shard_map/all_gather | solution.py:51
  123.7 5.5 %convert_bitcast_fusion = (bf16[1,1024,128]{1,2,0:T(8,128)(2,1)S(1)}, f32[1024]{0:T(1024)S(1)}) fusion(bf16[1,1024,128]{1,2,0:T(8,128)(2,1)S(1)} %copy.30, bf16[1024,3584]{1,0:T(8,128)(2,1)} %all-gather.2.cloned.1.call-done, bf16[1,128,3584]{2,1,0:T(8,128)(2,1)S(1)} %copy-done.2), kind=kOutput, calls=%fused_computation.17 | convolution fusion | flops 940047360 | bytes 8785920 | tf_op jit(solution)/shard_map/dot_general | solution.py:56
  129.2 13.2 %psum.7 = f32[8,128]{1,0:T(8,128)S(1)} all-reduce(f32[8,128]{1,0:T(8,128)S(1)} %bitcast.41), channel_id=1, replica_groups=mesh['node'=64,'local'=8] {'local'}, use_global_device_ids=true, to_apply=%region_6.7 | all-reduce | flops 1024 | bytes 8192 | tf_op jit(solution)/shard_map/psum | solution.py:70
  142.4 0.7 all_to_all.10
  143.2 15.8 %all-to-all-start.1 = ((f32[64,1,2]{2,1,0:T(1,128)}), f32[64,1,2]{2,1,0:T(1,128)S(1)}, u32[]{:S(2)}, u32[]{:S(2)}) async-start(f32[64,1,2]{2,1,0:T(1,128)} %bitcast.3), calls=%async_computation.1 | async-start | bytes 65536 | tf_op jit(solution)/shard_map/all_to_all | solution.py:72
  158.9 0.0 copy-done.3
  158.9 7.2 %fusion.6 = (bf16[1,128,3584]{1,2,0:T(8,128)(2,1)}, bf16[1,128,3584]{1,2,0:T(8,128)(2,1)S(1)}) fusion(bf16[1,128,3584]{1,2,0:T(8,128)(2,1)S(1)} %copy-done.3, bf16[1,128,3584]{1,2,0:T(8,128)(2,1)} %copy.29, bf16[1024,3584]{1,0:T(8,128)(2,1)} %all-gather.2.cloned.1.call-done, bf16[1,1024,128]{2,1,0:T(8,128)(2,1)S(1)} %copy-done.4), kind=kOutput, calls=%fused_computation.11 | convolution fusion | flops 946405376 | bytes 11272192 | tf_op jit(solution)/shard_map/dot_general | solution.py:60
  166.1 0.8 copy.33
  167.0 0.0 copy-start.6
  167.0 2.2 %copy.35 = bf16[1,128,3584]{2,1,0:T(8,128)(2,1)} copy(bf16[1,128,3584]{1,2,0:T(8,128)(2,1)} %get-tuple-element.22) | data formatting | bytes 1835008
  169.2 1.3 copy.34
  170.5 1.8 %all-to-all-done.1 = f32[64,1,2]{2,1,0:T(1,128)S(1)} async-done(((f32[64,1,2]{2,1,0:T(1,128)}), f32[64,1,2]{2,1,0:T(1,128)S(1)}, u32[]{:S(2)}, u32[]{:S(2)}) %all-to-all-start.1) | async-done | bytes 544 | tf_op jit(solution)/shard_map/all_to_all | solution.py:72
  172.3 0.5 broadcast.39
  172.8 0.7 reduce.7
  173.5 0.1 broadcast_in_dim.70
  173.7 0.1 select_reduce_fusion
  173.8 0.0 copy-done.6
  173.8 0.6 broadcast_select_fusion
  (5 shorter events, 0.1 us)
Async XLA Ops:
  7.2 2.1 %copy-start = (bf16[128,3584]{1,0:T(8,128)(2,1)S(1)}, bf16[128,3584]{1,0:T(8,128)(2,1)}, u32[]{:S(2)}) copy-start(bf16[128,3584]{1,0:T(8,128)(2,1)} %param.6) | copy-start | bytes 2752516
  7.2 116.5 %all-gather.2.cloned.1.call-start = ((), (), s32[]{:S(2)}) async-start(), calls=%async_computation.2 | async-start | bytes 8257536 | tf_op jit(solution)/shard_map/all_gather | solution.py:51
  8.7 0.6 copy-start.5
  77.0 1.3 copy-start.4
  77.0 1.5 copy-start.1
  78.3 1.5 copy-start.2
  81.0 77.9 %copy-start.3 = (bf16[1,128,3584]{1,2,0:T(8,128)(2,1)S(1)}, bf16[1,128,3584]{1,2,0:T(8,128)(2,1)}, u32[]{:S(2)}) copy-start(bf16[1,128,3584]{1,2,0:T(8,128)(2,1)} %copy.32) | copy-start | bytes 2752516
  143.2 29.1 %all-to-all-start.1 = ((f32[64,1,2]{2,1,0:T(1,128)}), f32[64,1,2]{2,1,0:T(1,128)S(1)}, u32[]{:S(2)}, u32[]{:S(2)}) async-start(f32[64,1,2]{2,1,0:T(1,128)} %bitcast.3), calls=%async_computation.1 | async-start | bytes 65536 | tf_op jit(solution)/shard_map/all_to_all | solution.py:72
  167.0 6.8 %copy-start.6 = (bf16[128]{0:T(256)(128)(2,1)S(1)}, bf16[128]{0:T(256)(128)(2,1)}, u32[]{:S(2)}) copy-start(bf16[128]{0:T(256)(128)(2,1)} %copy-done.5) | copy-start | bytes 772
Sparse Core Ops, SparseCore 0:
  78.4 45.2 all-gather.1
where the time goes:
time: 182 us; the launch traced here: 181 us
  blocking collectives  80.1 us (44%)
  waiting for transfers between devices  44.5 us (24%)
  starting transfers between devices  15.8 us (9%)
  between operations  14.2 us (8%)
  matrix products  13.1 us (7%)
  local copies, waits for them, and re-layouts  10.3 us (6%)
  other arithmetic  3.23 us (2%)
    all_to_all x1, blocking collectives, on_device(): lax.all_to_all(scaled_out.reshape(node_count, CAP, feature_count), 'node'...  66.9 us
    all_gather x1, waiting for transfers between devices, on_device(): lax.all_gather(arrived.reshape(node_count * CAP, feature_count), 'local',...  42.7 us
    all_to_all x1, starting transfers between devices, on_device(): lax.all_to_all(own_terms.reshape(node_count, CAP), 'node', split_axis=0,...  15.8 us
    psum x1, blocking collectives, on_device(): summed = lax.psum(score_terms, 'local')  13.2 us
    unnamed x20, local copies, waits for them, and re-layouts  7.28 us
    dot_general x1, matrix products, on_device(): lax.dot_general(hidden_now, scaled, (((0,), (0,)), ((), ())), preferred_e...  7.21 us
    dot_general x1, matrix products, on_device(): lax.dot_general(scaled, weight_now, (((1,), (1,)), ((), ())), preferred_e...  5.51 us
  transfers between devices with their start and end apart: 2, of which 2 were waited for; matrix products, arithmetic and copies ran while one was open for 8% of the time, Pallas kernels for 0%

commit v1 on v0

--- a/solution.py
+++ b/solution.py
@@ -48,9 +48,36 @@
         concat_axis=0,
         tiled=True,
     )
-    scaled = lax.all_gather(
-        arrived.reshape(node_count * CAP, feature_count), "local", axis=0, tiled=True
-    )
+
+    def render_desk(x_part, axis_key):
+        carry, w1, back = (
+            jax.lax.axis_size(axis_key),
+            jax.lax.axis_index(axis_key),
+            x_part.shape[0],
+        )
+        low = lax.dynamic_update_slice_in_dim(
+            jnp.zeros(
+                [idx * carry if tick == 0 else idx for tick, idx in enumerate(x_part.shape)],
+                x_part.dtype,
+            ),
+            x_part,
+            w1 * back,
+            axis=0,
+        )
+        s_next = opened = x_part
+        for no in tuple(range(1, carry // 2 + 1)):
+            s_next = jax.lax.ppermute(
+                s_next, axis_key, [(tick, (tick + 1) % carry) for tick in range(carry)]
+            )
+            low = lax.dynamic_update_slice_in_dim(low, s_next, (w1 - no) % carry * back, axis=0)
+            if 2 * no < carry:
+                opened = jax.lax.ppermute(
+                    opened, axis_key, [(tick, (tick - 1) % carry) for tick in range(carry)]
+                )
+                low = lax.dynamic_update_slice_in_dim(low, opened, (w1 + no) % carry * back, axis=0)
+        return low
+
+    scaled = render_desk(arrived.reshape(node_count * CAP, feature_count), "local")
     weight_now = down_weight[0]
     hidden_now = saved_hidden[0]
     hidden_f = lax.dot_general(

time: 182 us -> 169 us (0.929)
  the two profiles are of different devices: /device:TPU:8 before, /device:TPU:1 now
where the time goes in v1:
time: 169 us; the launch traced here: 168 us
  blocking collectives  82.6 us (49%)
  waiting for transfers between devices  33.6 us (20%)
  starting transfers between devices  19.9 us (12%)
  local copies, waits for them, and re-layouts  17.7 us (10%)
  matrix products  10.1 us (6%)
  other arithmetic  3.25 us (2%)
    all_to_all x1, blocking collectives, on_device(): lax.all_to_all(scaled_out.reshape(node_count, CAP, feature_count), 'node'...  64.6 us
    ppermute x4, waiting for transfers between devices, render_desk(): jax.lax.ppermute(s_next, axis_key, [(tick, (tick + 1) % carry) for tick i...  32.3 us
    psum x1, blocking collectives, on_device(): summed = lax.psum(score_terms, 'local')  18 us
    ppermute x4, starting transfers between devices, render_desk(): jax.lax.ppermute(s_next, axis_key, [(tick, (tick + 1) % carry) for tick i...  12.5 us
    unnamed x20, local copies, waits for them, and re-layouts  12.2 us
    dot_general x1, matrix products, on_device(): lax.dot_general(hidden_now, scaled, (((0,), (0,)), ((), ())), preferred_e...  7.32 us
    all_to_all x1, starting transfers between devices, on_device(): lax.all_to_all(own_terms.reshape(node_count, CAP), 'node', split_axis=0,...  6.25 us
  transfers between devices with their start and end apart: 8, of which 7 were waited for; matrix products, arithmetic and copies ran while one was open for 12% of the time, Pallas kernels for 0%

profile of v1, /device:TPU:1, one launch (start us, length us, event | category | flops | bytes accessed | tf_op | source)
XLA Modules:
  0.0 168.1 jit_solution(9749196867345817361)
XLA Ops:
  0.6 0.0 copy-start
  0.6 0.0 copy-start.4
  0.7 0.8 fusion.18
  1.5 0.2 convert_reduce_fusion
  1.7 0.7 select_reduce_fusion.2
  2.4 0.0 copy-start.5
  2.4 0.1 select_reduce_fusion.1
  2.5 0.0 copy-done
  2.5 0.4 fusion
  2.9 0.3 reshape.51
  3.3 64.6 %all_to_all.14 = bf16[64,2,3584]{2,1,0:T(2,128)(2,1)S(1)} all-to-all(bf16[64,2,3584]{2,1,0:T(2,128)(2,1)S(1)} %reshape.51), channel_id=1, replica_groups=mesh['node'=64,'local'=8] {'node'}, dimensions={0} | all-to-all | bytes 1835008 | tf_op jit(solution)/shard_map/all_to_all | solution.py:44
  67.8 0.3 reshape.52
  68.2 5.1 %collective-permute-start = (bf16[128,3584]{1,0:T(8,128)(2,1)S(1)}, bf16[128,3584]{1,0:T(8,128)(2,1)}, u32[]{:S(2)}, u32[]{:S(2)}) collective-permute-start(bf16[128,3584]{1,0:T(8,128)(2,1)S(1)} %reshape.52), channel_id=1, source_target_pairs={{0,1},{1,2},{2,3},{3,4},{4,5},{5,6},{6,7},{7,0},{8,9},{9,10},{10,1... | collective-permute-start | bytes 2752520 | tf_op jit(solution)/shard_map/ppermute | solution.py:69
  73.2 0.0 collective-permute-start.1
  73.2 1.5 copy.29
  74.8 0.0 copy-done.5
  74.8 2.2 %copy.32 = bf16[1,128,3584]{1,2,0:T(8,128)(2,1)} copy(bf16[1,128,3584]{2,1,0:T(8,128)(2,1)} %param.11) | data formatting | bytes 1835008 | tf_op args[5]
  77.0 0.0 copy-done.4
  77.0 0.1 copy.30
  77.2 0.5 broadcast_in_dim.70
  77.7 0.0 copy-start.2
  77.7 0.1 constant_dynamic-update-slice_fusion.7
  77.8 5.8 %collective-permute-done = bf16[128,3584]{1,0:T(8,128)(2,1)} collective-permute-done((bf16[128,3584]{1,0:T(8,128)(2,1)S(1)}, bf16[128,3584]{1,0:T(8,128)(2,1)}, u32[]{:S(2)}, u32[]{:S(2)}) %collective-permute-start) | collective-permute-done | bytes 917536 | tf_op jit(solution)/shard_map/ppermute | solution.py:69
  83.6 2.6 %collective-permute-start.2 = (bf16[128,3584]{1,0:T(8,128)(2,1)}, bf16[128,3584]{1,0:T(8,128)(2,1)S(1)}, u32[]{:S(2)}, u32[]{:S(2)}) collective-permute-start(bf16[128,3584]{1,0:T(8,128)(2,1)} %collective-permute-done), channel_id=1, source_target_pairs={{0,1},{1,2},{2,3},{3,4},{4,5},{5,6},{6,7},{7,0},{8,9},{9,10},{10,1... | collective-permute-start | bytes 2752520 | tf_op jit(solution)/shard_map/ppermute | solution.py:69
  86.2 0.0 collective-permute-done.1
  86.2 0.1 collective-permute-start.3
  86.3 1.3 constant_dynamic-update-slice_fusion.6
  87.5 1.3 constant_dynamic-update-slice_fusion.5
  88.8 8.0 %collective-permute-done.2 = bf16[128,3584]{1,0:T(8,128)(2,1)S(1)} collective-permute-done((bf16[128,3584]{1,0:T(8,128)(2,1)}, bf16[128,3584]{1,0:T(8,128)(2,1)S(1)}, u32[]{:S(2)}, u32[]{:S(2)}) %collective-permute-start.2) | collective-permute-done | bytes 917536 | tf_op jit(solution)/shard_map/ppermute | solution.py:69
  96.8 2.4 %collective-permute-start.4 = (bf16[128,3584]{1,0:T(8,128)(2,1)S(1)}, bf16[128,3584]{1,0:T(8,128)(2,1)S(1)}, u32[]{:S(2)}, u32[]{:S(2)}) collective-permute-start(bf16[128,3584]{1,0:T(8,128)(2,1)S(1)} %collective-permute-done.2), channel_id=1, source_target_pairs={{0,1},{1,2},{2,3},{3,4},{4,5},{5,6},{6,7},{7,0},{8,9},{9,10},{10,1... | collective-permute-start | bytes 2752520 | tf_op jit(solution)/shard_map/ppermute | solution.py:69
  99.2 0.3 collective-permute-done.3
  99.5 1.0 collective-permute-start.5
  100.5 0.1 constant_dynamic-update-slice_fusion.4
  100.6 0.1 constant_dynamic-update-slice_fusion.3
  100.7 8.8 %collective-permute-done.4 = bf16[128,3584]{1,0:T(8,128)(2,1)S(1)} collective-permute-done((bf16[128,3584]{1,0:T(8,128)(2,1)S(1)}, bf16[128,3584]{1,0:T(8,128)(2,1)S(1)}, u32[]{:S(2)}, u32[]{:S(2)}) %collective-permute-start.4) | collective-permute-done | bytes 917536 | tf_op jit(solution)/shard_map/ppermute | solution.py:69
  109.5 2.5 %collective-permute-start.6 = (bf16[128,3584]{1,0:T(8,128)(2,1)S(1)}, bf16[128,3584]{1,0:T(8,128)(2,1)S(1)}, u32[]{:S(2)}, u32[]{:S(2)}) collective-permute-start(bf16[128,3584]{1,0:T(8,128)(2,1)S(1)} %collective-permute-done.4), channel_id=1, source_target_pairs={{0,1},{1,2},{2,3},{3,4},{4,5},{5,6},{6,7},{7,0},{8,9},{9,10},{10,1... | collective-permute-start | bytes 2752520 | tf_op jit(solution)/shard_map/ppermute | solution.py:69
  112.0 0.1 constant_dynamic-update-slice_fusion.2
  112.1 0.0 copy-start.3
  112.1 0.5 collective-permute-done.5
  112.6 0.1 constant_dynamic-update-slice_fusion.1
  112.7 9.7 %collective-permute-done.6 = bf16[128,3584]{1,0:T(8,128)(2,1)S(1)} collective-permute-done((bf16[128,3584]{1,0:T(8,128)(2,1)S(1)}, bf16[128,3584]{1,0:T(8,128)(2,1)S(1)}, u32[]{:S(2)}, u32[]{:S(2)}) %collective-permute-start.6) | collective-permute-done | bytes 917536 | tf_op jit(solution)/shard_map/ppermute | solution.py:69
  122.3 0.1 constant_dynamic-update-slice_fusion
  122.4 0.0 copy-start.1
  122.4 3.0 %copy-done.1 = bf16[1024,3584]{1,0:T(8,128)(2,1)} copy-done((bf16[1024,3584]{1,0:T(8,128)(2,1)}, bf16[1024,3584]{1,0:T(8,128)(2,1)S(1)}, u32[]{:S(2)}) %copy-start.1) | copy-done | bytes 7340056
  125.4 0.0 copy-done.2
  125.4 2.4 %convert_bitcast_fusion = (bf16[1,1024,128]{1,2,0:T(8,128)(2,1)S(1)}, f32[1024]{0:T(1024)S(1)}) fusion(bf16[1,1024,128]{1,2,0:T(8,128)(2,1)S(1)} %copy.30, bf16[1024,3584]{1,0:T(8,128)(2,1)S(1)} %constant_dynamic-update-slice_fusion, bf16[1,128,3584]{2,1,0:T(8,128)(2,1)S(1)} %copy-done.2), kind=kOutput, calls=%fused_computation.17 | convolution fusion | flops 940047360 | bytes 8785920 | tf_op jit(solution)/shard_map/dot_general | solution.py:83
  127.8 18.0 %psum.7 = f32[8,128]{1,0:T(8,128)S(1)} all-reduce(f32[8,128]{1,0:T(8,128)S(1)} %bitcast.41), channel_id=1, replica_groups=mesh['node'=64,'local'=8] {'local'}, use_global_device_ids=true, to_apply=%region_6.7 | all-reduce | flops 1024 | bytes 8192 | tf_op jit(solution)/shard_map/psum | solution.py:97
  145.9 0.7 all_to_all.10
  146.6 6.2 %all-to-all-start.1 = ((f32[64,1,2]{2,1,0:T(1,128)}), f32[64,1,2]{2,1,0:T(1,128)S(1)}, u32[]{:S(2)}, u32[]{:S(2)}) async-start(f32[64,1,2]{2,1,0:T(1,128)} %bitcast.3), calls=%async_computation.1 | async-start | bytes 65536 | tf_op jit(solution)/shard_map/all_to_all | solution.py:99
  152.9 0.0 copy-done.3
  152.9 0.0 copy-start.6
  152.9 7.3 %fusion.6 = (bf16[1,128,3584]{1,2,0:T(8,128)(2,1)}, bf16[1,128,3584]{1,2,0:T(8,128)(2,1)}) fusion(bf16[1,128,3584]{1,2,0:T(8,128)(2,1)S(1)} %copy-done.3, bf16[1,128,3584]{1,2,0:T(8,128)(2,1)S(1)} %copy.29, bf16[1024,3584]{1,0:T(8,128)(2,1)} %copy-done.1, bf16[1,1024,128]{2,1,0:T(8,128)(2,1)S(1)} %copy-done.4), kind=kOutput, calls=%fused_computation.11 | convolution fusion | flops 946405376 | bytes 11272192 | tf_op jit(solution)/shard_map/dot_general | solution.py:87
  160.2 2.2 %copy.34 = bf16[1,128,3584]{2,1,0:T(8,128)(2,1)} copy(bf16[1,128,3584]{1,2,0:T(8,128)(2,1)} %get-tuple-element.23) | data formatting | bytes 1835008
  162.4 2.2 %copy.35 = bf16[1,128,3584]{2,1,0:T(8,128)(2,1)} copy(bf16[1,128,3584]{1,2,0:T(8,128)(2,1)} %get-tuple-element.22) | data formatting | bytes 1835008
  164.6 0.8 copy.33
  165.5 0.5 all-to-all-done.1
  166.0 0.5 broadcast.50
  166.5 0.7 reduce.7
  167.2 0.1 broadcast_in_dim.74
  167.4 0.1 select_reduce_fusion
  167.5 0.0 copy-done.6
  167.5 0.6 broadcast_select_fusion
  (5 shorter events, 0.1 us)
Async XLA Ops:
  0.6 1.9 %copy-start = (bf16[128,3584]{1,0:T(8,128)(2,1)S(1)}, bf16[128,3584]{1,0:T(8,128)(2,1)}, u32[]{:S(2)}) copy-start(bf16[128,3584]{1,0:T(8,128)(2,1)} %param.6) | copy-start | bytes 2752516
  0.6 76.4 %copy-start.4 = (bf16[1,1024,128]{2,1,0:T(8,128)(2,1)S(1)}, bf16[1,1024,128]{2,1,0:T(8,128)(2,1)}, u32[]{:S(2)}) copy-start(bf16[1,1024,128]{2,1,0:T(8,128)(2,1)} %param.9) | copy-start | bytes 786436
  2.4 72.4 %copy-start.5 = (bf16[128]{0:T(256)(128)(2,1)}, bf16[128]{0:T(256)(128)(2,1)S(1)}, u32[]{:S(2)}) copy-start(bf16[128]{0:T(256)(128)(2,1)S(1)} %select_reduce_fusion.2) | copy-start | bytes 772
  68.2 15.4 %collective-permute-start = (bf16[128,3584]{1,0:T(8,128)(2,1)S(1)}, bf16[128,3584]{1,0:T(8,128)(2,1)}, u32[]{:S(2)}, u32[]{:S(2)}) collective-permute-start(bf16[128,3584]{1,0:T(8,128)(2,1)S(1)} %reshape.52), channel_id=1, source_target_pairs={{0,1},{1,2},{2,3},{3,4},{4,5},{5,6},{6,7},{7,0},{8,9},{9,10},{10,1... | collective-permute-start | bytes 2752520 | tf_op jit(solution)/shard_map/ppermute | solution.py:69
  73.2 12.9 %collective-permute-start.1 = (bf16[128,3584]{1,0:T(8,128)(2,1)S(1)}, bf16[128,3584]{1,0:T(8,128)(2,1)}, u32[]{:S(2)}, u32[]{:S(2)}) collective-permute-start(bf16[128,3584]{1,0:T(8,128)(2,1)S(1)} %reshape.52), channel_id=1, source_target_pairs={{0,7},{1,0},{2,1},{3,2},{4,3},{5,4},{6,5},{7,6},{8,15},{9,8},{10,9... | collective-permute-start | bytes 2752520 | tf_op jit(solution)/shard_map/ppermute | solution.py:74
  77.7 47.7 %copy-start.2 = (bf16[1,128,3584]{2,1,0:T(8,128)(2,1)S(1)}, bf16[1,128,3584]{2,1,0:T(8,128)(2,1)}, u32[]{:S(2)}) copy-start(bf16[1,128,3584]{2,1,0:T(8,128)(2,1)} %param.10) | copy-start | bytes 2752516
  83.6 13.2 %collective-permute-start.2 = (bf16[128,3584]{1,0:T(8,128)(2,1)}, bf16[128,3584]{1,0:T(8,128)(2,1)S(1)}, u32[]{:S(2)}, u32[]{:S(2)}) collective-permute-start(bf16[128,3584]{1,0:T(8,128)(2,1)} %collective-permute-done), channel_id=1, source_target_pairs={{0,1},{1,2},{2,3},{3,4},{4,5},{5,6},{6,7},{7,0},{8,9},{9,10},{10,1... | collective-permute-start | bytes 2752520 | tf_op jit(solution)/shard_map/ppermute | solution.py:69
  86.2 13.3 %collective-permute-start.3 = (bf16[128,3584]{1,0:T(8,128)(2,1)}, bf16[128,3584]{1,0:T(8,128)(2,1)S(1)}, u32[]{:S(2)}, u32[]{:S(2)}) collective-permute-start(bf16[128,3584]{1,0:T(8,128)(2,1)} %collective-permute-done.1), channel_id=1, source_target_pairs={{0,7},{1,0},{2,1},{3,2},{4,3},{5,4},{6,5},{7,6},{8,15},{9,8},{10,9... | collective-permute-start | bytes 2752520 | tf_op jit(solution)/shard_map/ppermute | solution.py:74
  96.8 12.7 %collective-permute-start.4 = (bf16[128,3584]{1,0:T(8,128)(2,1)S(1)}, bf16[128,3584]{1,0:T(8,128)(2,1)S(1)}, u32[]{:S(2)}, u32[]{:S(2)}) collective-permute-start(bf16[128,3584]{1,0:T(8,128)(2,1)S(1)} %collective-permute-done.2), channel_id=1, source_target_pairs={{0,1},{1,2},{2,3},{3,4},{4,5},{5,6},{6,7},{7,0},{8,9},{9,10},{10,1... | collective-permute-start | bytes 2752520 | tf_op jit(solution)/shard_map/ppermute | solution.py:69
  99.5 13.1 %collective-permute-start.5 = (bf16[128,3584]{1,0:T(8,128)(2,1)S(1)}, bf16[128,3584]{1,0:T(8,128)(2,1)S(1)}, u32[]{:S(2)}, u32[]{:S(2)}) collective-permute-start(bf16[128,3584]{1,0:T(8,128)(2,1)S(1)} %collective-permute-done.3), channel_id=1, source_target_pairs={{0,7},{1,0},{2,1},{3,2},{4,3},{5,4},{6,5},{7,6},{8,15},{9,8},{10,9... | collective-permute-start | bytes 2752520 | tf_op jit(solution)/shard_map/ppermute | solution.py:74
  109.5 12.8 %collective-permute-start.6 = (bf16[128,3584]{1,0:T(8,128)(2,1)S(1)}, bf16[128,3584]{1,0:T(8,128)(2,1)S(1)}, u32[]{:S(2)}, u32[]{:S(2)}) collective-permute-start(bf16[128,3584]{1,0:T(8,128)(2,1)S(1)} %collective-permute-done.4), channel_id=1, source_target_pairs={{0,1},{1,2},{2,3},{3,4},{4,5},{5,6},{6,7},{7,0},{8,9},{9,10},{10,1... | collective-permute-start | bytes 2752520 | tf_op jit(solution)/shard_map/ppermute | solution.py:69
  112.1 40.8 %copy-start.3 = (bf16[1,128,3584]{1,2,0:T(8,128)(2,1)S(1)}, bf16[1,128,3584]{1,2,0:T(8,128)(2,1)}, u32[]{:S(2)}) copy-start(bf16[1,128,3584]{1,2,0:T(8,128)(2,1)} %copy.32) | copy-start | bytes 2752516
  122.4 3.0 %copy-start.1 = (bf16[1024,3584]{1,0:T(8,128)(2,1)}, bf16[1024,3584]{1,0:T(8,128)(2,1)S(1)}, u32[]{:S(2)}) copy-start(bf16[1024,3584]{1,0:T(8,128)(2,1)S(1)} %constant_dynamic-update-slice_fusion) | copy-start | bytes 22020100
  146.6 19.4 %all-to-all-start.1 = ((f32[64,1,2]{2,1,0:T(1,128)}), f32[64,1,2]{2,1,0:T(1,128)S(1)}, u32[]{:S(2)}, u32[]{:S(2)}) async-start(f32[64,1,2]{2,1,0:T(1,128)} %bitcast.3), calls=%async_computation.1 | async-start | bytes 65536 | tf_op jit(solution)/shard_map/all_to_all | solution.py:99
  152.9 14.6 %copy-start.6 = (bf16[128]{0:T(256)(128)(2,1)S(1)}, bf16[128]{0:T(256)(128)(2,1)}, u32[]{:S(2)}) copy-start(bf16[128]{0:T(256)(128)(2,1)} %copy-done.5) | copy-start | bytes 772
